TPU v7x, 256 devices: a whole 4x4x8 slice. The times are simulated.
256 devices in a mesh: seq: 8 (over z), head: 32 (over y, x, core).
Axes of the slice: x: 4, y: 4, z: 8, core: 2. Of those that a mesh axis runs over, the one named last changes fastest.
Arguments:
- queries: bfloat16 [4096, 32, 128], P(('seq', 'head')), may hold values from -6 to 6
- keys: bfloat16 [4096, 32, 128], P(('seq', 'head')), may hold values from -6 to 6
- values: bfloat16 [4096, 32, 128], P(('seq', 'head')), may hold values from -6 to 6
- out_grad: bfloat16 [4096, 32, 128], P(('seq', 'head')), may hold values from -1.5 to 1.5
- level_weights: float32 [32, 13, 4096], P('head', None, 'seq'), may hold values from 0.2 to 2
Outputs:
- query_grad: bfloat16 [4096, 32, 128], P(('seq', 'head'))
- key_grad: bfloat16 [4096, 32, 128], P(('seq', 'head'))
- value_grad: bfloat16 [4096, 32, 128], P(('seq', 'head'))
- weight_grad: float32 [32, 13, 4096], P('head', None, 'seq')
All inputs are finite; a program needn't handle non-finite values.
Results may differ from a plain program's by a relative error of at most 0.0052.
Values may be sent and summed in bfloat16 or wider, within the bound.
No kernel may reach another device: no remote copies, remote signals or barrier semaphores. Data moves between devices by JAX's collectives and lax.ppermute only.
A program may use at most 64 MiB of HBM per device.

v0:
```python
import math

import jax
import jax.numpy as jnp
from jax import lax
from jax.sharding import PartitionSpec as P


def partner(value, axis, apart):
    mask = 2**apart
    pairs = [(source, source ^ mask) for source in range(lax.axis_size(axis))]
    return lax.ppermute(value, axis, pairs)


def bit_length(values, number):
    running = jnp.zeros(values.shape, jnp.int32)
    for exponent in range(number):
        running = running + (values >= 2**exponent).astype(jnp.int32)
    return running


def level_factor(degree, head_width):
    base_scale = 1.0 / math.sqrt(head_width)
    if degree == 0:
        return base_scale
    return base_scale * 2.0 ** (-(degree - 1) / 2.0)


def spread_states(lower_source, upper_source):
    far_count = lax.axis_size("seq").bit_length() - 1
    position = lax.axis_index("seq")
    lower_states = []
    upper_states = []
    offset = 1
    running = lower_source
    pending = list(upper_source)
    for degree in range(far_count):
        outgoing = [running] + pending[degree:]
        received = partner(jnp.stack(outgoing), "seq", degree)
        upper_bit = position // 2**degree % 2 == 1
        lower_states.append(jnp.where(upper_bit, received[0], 0.0))
        running = running + received[0]
        upper_states.append(jnp.where(upper_bit, 0.0, received[offset]))
        for later_level in range(degree + 1, far_count):
            pending[later_level] = pending[later_level] + received[offset + later_level - degree]
    return (lower_states, upper_states)


def query_states(query_rows, grad_rows, level_weights, first_far):
    head_width = query_rows.shape[2]
    far_count = level_weights.shape[1] - first_far
    coefficients = jnp.stack(
        [
            level_factor(first_far + degree, head_width) * level_weights[:, first_far + degree, :]
            for degree in range(far_count)
        ]
    )
    scaled = (jnp.transpose(coefficients, (0, 2, 1))[..., None] * grad_rows[None]).astype(
        jnp.bfloat16
    )
    states = jnp.einsum("thd,jthe->jhde", query_rows, scaled, preferred_element_type=jnp.float32)
    return (coefficients, [states[degree] for degree in range(far_count)])


def near_terms(query_rows, key_rows, value_rows, grad_rows, level_weights):
    tok_count = query_rows.shape[0]
    heads_here = query_rows.shape[1]
    head_width = query_rows.shape[2]
    block_rows = min(512, tok_count)
    block_bits = block_rows.bit_length() - 1
    local_bits = tok_count.bit_length() - 1
    pieces = tok_count // block_rows
    zero_block = jnp.zeros((block_rows, heads_here, head_width), jnp.float32)
    zero_weights = jnp.zeros((heads_here, block_rows), jnp.float32)
    query_parts = [zero_block] * pieces
    key_parts = [zero_block] * pieces
    value_parts = [zero_block] * pieces
    weight_rows = [[zero_weights] * pieces for degree in range(local_bits + 1)]
    positions = jnp.arange(block_rows, dtype=jnp.int32)
    crossed = jnp.bitwise_xor(positions[:, None], positions[None, :])
    causal = positions[None, :] <= positions[:, None]
    inside = bit_length(crossed, block_bits)
    scores = jnp.einsum("thd,shd->hts", query_rows, key_rows, preferred_element_type=jnp.float32)
    pulls = jnp.einsum("the,she->hts", grad_rows, value_rows, preferred_element_type=jnp.float32)
    product = jnp.where(causal[None], scores * pulls, 0.0)
    weights = jnp.zeros(scores.shape, jnp.float32)
    for degree in range(block_bits + 1):
        factor = level_factor(degree, head_width)
        matching = (causal & (inside == degree))[None]
        column = (factor * level_weights[:, degree, :])[:, :, None]
        weights = jnp.where(matching, column, weights)
        chosen = jnp.sum(jnp.where(matching, product, 0.0), axis=2)
        weight_rows[degree][0] = factor * chosen
    near_scaled = (weights * scores).astype(jnp.bfloat16)
    near_pulled = (weights * pulls).astype(jnp.bfloat16)
    value_parts[0] = jnp.einsum(
        "hts,the->she", near_scaled, grad_rows, preferred_element_type=jnp.float32
    )
    query_parts[0] = jnp.einsum(
        "hts,shd->thd", near_pulled, key_rows, preferred_element_type=jnp.float32
    )
    key_parts[0] = jnp.einsum(
        "hts,thd->shd", near_pulled, query_rows, preferred_element_type=jnp.float32
    )
    weight_near = [jnp.concatenate(weight_rows[degree], axis=1) for degree in range(local_bits + 1)]
    return (query_parts[0], key_parts[0], value_parts[0], weight_near)


def on_device(queries, keys, values, out_grad, level_weights):
    query_rows, key_rows, value_rows, grad_rows = (
        lax.all_to_all(queries, "head", split_axis=1, concat_axis=0, tiled=True),
        lax.all_to_all(keys, "head", split_axis=1, concat_axis=0, tiled=True),
        lax.all_to_all(values, "head", split_axis=1, concat_axis=0, tiled=True),
        lax.all_to_all(out_grad, "head", split_axis=1, concat_axis=0, tiled=True),
    )
    first_far = query_rows.shape[0].bit_length()
    key_state = jnp.einsum("shd,she->hde", key_rows, value_rows, preferred_element_type=jnp.float32)
    coefficients, upper_parts = query_states(query_rows, grad_rows, level_weights, first_far)
    lower_states, upper_states = spread_states(key_state, upper_parts)
    head_width = query_rows.shape[2]
    far_count = level_weights.shape[1] - first_far
    query_near, key_near, value_near, weight_near = near_terms(
        query_rows, key_rows, value_rows, grad_rows, level_weights
    )
    lower_narrow = jnp.stack([matrix.astype(jnp.bfloat16) for matrix in lower_states])
    far_update = jnp.einsum(
        "the,jhde->jthd", grad_rows, lower_narrow, preferred_element_type=jnp.float32
    )
    query_total = query_near + jnp.sum(
        jnp.transpose(coefficients, (0, 2, 1))[..., None] * far_update, axis=0
    )
    upper_total = upper_states[0]
    for degree in range(1, far_count):
        upper_total = upper_total + upper_states[degree]
    upper_narrow = upper_total.astype(jnp.bfloat16)
    key_total = key_near + jnp.einsum(
        "she,hde->shd", value_rows, upper_narrow, preferred_element_type=jnp.float32
    )
    value_total = value_near + jnp.einsum(
        "shd,hde->she", key_rows, upper_narrow, preferred_element_type=jnp.float32
    )
    factors = jnp.array(
        [level_factor(first_far + degree, head_width) for degree in range(far_count)], jnp.float32
    )
    weight_far = factors[:, None, None] * jnp.sum(query_rows[None] * far_update, axis=-1)
    weight_grad = jnp.stack(
        weight_near + [weight_far[degree].T for degree in range(far_count)], axis=1
    )
    query_out, key_out, value_out = (
        lax.all_to_all(
            query_total.astype(jnp.bfloat16), "head", split_axis=0, concat_axis=1, tiled=True
        ),
        lax.all_to_all(
            key_total.astype(jnp.bfloat16), "head", split_axis=0, concat_axis=1, tiled=True
        ),
        lax.all_to_all(
            value_total.astype(jnp.bfloat16), "head", split_axis=0, concat_axis=1, tiled=True
        ),
    )
    return (query_out, key_out, value_out, weight_grad)


def solution(mesh):
    in_specs = (
        P(("seq", "head"), None, None),
        P(("seq", "head"), None, None),
        P(("seq", "head"), None, None),
        P(("seq", "head"), None, None),
        P("head", None, "seq"),
    )
    out_specs = (
        P(("seq", "head"), None, None),
        P(("seq", "head"), None, None),
        P(("seq", "head"), None, None),
        P("head", None, "seq"),
    )
    return jax.shard_map(
        on_device, mesh=mesh, in_specs=in_specs, out_specs=out_specs, check_vma=False
    )
```

profile of v0, /device:TPU:1, one launch (start us, length us, event | category | flops | bytes accessed | tf_op | source)
XLA Modules:
  0.0 130.0 jit_solution(8321953172399653575)
XLA Ops:
  0.6 1.6 %copy.54 = bf16[16,32,128]{2,0,1:T(8,128)(2,1)} copy(bf16[16,32,128]{2,1,0:T(8,128)(2,1)} %param.9) | data formatting | bytes 262144 | tf_op args[3]
  2.2 8.7 %all-to-all-start = ((bf16[16,32,128]{2,0,1:T(8,128)(2,1)}), bf16[16,32,128]{2,0,1:T(8,128)(2,1)S(1)}, u32[]{:S(2)}, u32[]{:S(2)}) async-start(bf16[16,32,128]{2,0,1:T(8,128)(2,1)} %copy.54), calls=%async_computation | async-start | bytes 262144 | tf_op jit(solution)/shard_map/all_to_all | solution.py:114
  11.0 0.7 copy.55
  11.7 6.9 %all-to-all-done = bf16[16,32,128]{2,0,1:T(8,128)(2,1)S(1)} async-done(((bf16[16,32,128]{2,0,1:T(8,128)(2,1)}), bf16[16,32,128]{2,0,1:T(8,128)(2,1)S(1)}, u32[]{:S(2)}, u32[]{:S(2)}) %all-to-all-start) | async-done | bytes 131104 | tf_op jit(solution)/shard_map/all_to_all | solution.py:114
  18.6 3.9 %all-to-all-start.1 = ((bf16[16,32,128]{2,0,1:T(8,128)(2,1)}), bf16[16,32,128]{2,0,1:T(8,128)(2,1)S(1)}, u32[]{:S(2)}, u32[]{:S(2)}) async-start(bf16[16,32,128]{2,0,1:T(8,128)(2,1)} %copy.55), calls=%async_computation.1 | async-start | bytes 262144 | tf_op jit(solution)/shard_map/all_to_all | solution.py:113
  22.5 0.7 copy.58
  23.2 7.0 %all-to-all-done.1 = bf16[16,32,128]{2,0,1:T(8,128)(2,1)S(1)} async-done(((bf16[16,32,128]{2,0,1:T(8,128)(2,1)}), bf16[16,32,128]{2,0,1:T(8,128)(2,1)S(1)}, u32[]{:S(2)}, u32[]{:S(2)}) %all-to-all-start.1) | async-done | bytes 131104 | tf_op jit(solution)/shard_map/all_to_all | solution.py:113
  30.2 3.9 %all-to-all-start.2 = ((bf16[16,32,128]{2,0,1:T(8,128)(2,1)}), bf16[16,32,128]{2,0,1:T(8,128)(2,1)S(1)}, u32[]{:S(2)}, u32[]{:S(2)}) async-start(bf16[16,32,128]{2,0,1:T(8,128)(2,1)} %copy.58), calls=%async_computation.2 | async-start | bytes 262144 | tf_op jit(solution)/shard_map/all_to_all | solution.py:112
  34.2 0.8 copy-done.2
  35.1 0.7 copy.62
  35.9 6.0 %all-to-all-done.2 = bf16[16,32,128]{2,0,1:T(8,128)(2,1)S(1)} async-done(((bf16[16,32,128]{2,0,1:T(8,128)(2,1)}), bf16[16,32,128]{2,0,1:T(8,128)(2,1)S(1)}, u32[]{:S(2)}, u32[]{:S(2)}) %all-to-all-start.2) | async-done | bytes 131104 | tf_op jit(solution)/shard_map/all_to_all | solution.py:112
  41.8 3.9 %all-to-all-start.3 = ((bf16[16,32,128]{2,0,1:T(8,128)(2,1)}), bf16[16,32,128]{2,0,1:T(8,128)(2,1)S(1)}, u32[]{:S(2)}, u32[]{:S(2)}) async-start(bf16[16,32,128]{2,0,1:T(8,128)(2,1)} %copy.62), calls=%async_computation.3 | async-start | bytes 262144 | tf_op jit(solution)/shard_map/all_to_all | solution.py:111
  46.2 7.3 %all-to-all-done.3 = bf16[16,32,128]{2,0,1:T(8,128)(2,1)S(1)} async-done(((bf16[16,32,128]{2,0,1:T(8,128)(2,1)}), bf16[16,32,128]{2,0,1:T(8,128)(2,1)S(1)}, u32[]{:S(2)}, u32[]{:S(2)}) %all-to-all-start.3) | async-done | bytes 131104 | tf_op jit(solution)/shard_map/all_to_all | solution.py:111
  53.5 1.7 %fusion.9 = (f32[512,512]{0,1:T(8,128)S(1)}, bf16[512,512]{0,1:T(8,128)(2,1)S(1)}, f32[512,512]{0,1:T(8,128)}) fusion(f32[512,512]{0,1:T(8,128)S(1)} %fusion.61, f32[512]{0:T(512)S(1)} %bitcast.184, f32[512]{0:T(512)S(1)} %bitcast.186, f32[512]{0:T(512)S(1)} %bitcast.188, f32[512]{0:T(512)S(1)} %bitcast.190, f32[512]{0:T(512)S(1)} %bitcast.192, ...), kind=kOutput, calls=%fused_computation.11 | convolution fusion | flops 83361792 | bytes 3952640 | tf_op jit(solution)/shard_map/thd,shd->hts/dot_general | solution.py:83
  55.2 3.1 %select_reduce_fusion = (f32[512]{0:T(512)S(1)}, f32[512]{0:T(512)S(1)}, f32[512]{0:T(512)S(1)}, f32[512]{0:T(512)S(1)}, f32[512]{0:T(512)S(1)}, /*index=5*/f32[...) fusion(f32[512,512]{0,1:T(8,128)S(1)} %get-tuple-element.28), kind=kLoop, calls=%fused_computation.35 | loop fusion | flops 17820672 | bytes 1069056 | tf_op jit(solution)/shard_map/reduce_sum | solution.py:92
  59.1 1.7 %collective-permute-start = (f32[4,1,128,128]{3,2,1,0:T(8,128)S(1)}, f32[4,1,128,128]{3,2,1,0:T(8,128)S(1)}, u32[]{:S(2)}, u32[]{:S(2)}) collective-permute-start(f32[4,1,128,128]{3,2,1,0:T(8,128)S(1)} %pad_maximum_fusion), channel_id=1, source_target_pairs={{0,32},{32,0},{64,96},{96,64},{128,160},{160,128},{192,224},{224,1... | collective-permute-start | bytes 786440 | tf_op jit(solution)/shard_map/ppermute | solution.py:12
  60.8 0.8 convolution_bitcast_fusion.1
  62.2 4.8 %collective-permute-done = f32[4,1,128,128]{3,2,1,0:T(8,128)S(1)} collective-permute-done((f32[4,1,128,128]{3,2,1,0:T(8,128)S(1)}, f32[4,1,128,128]{3,2,1,0:T(8,128)S(1)}, u32[]{:S(2)}, u32[]{:S(2)}) %collective-permute-start) | collective-permute-done | bytes 262176 | tf_op jit(solution)/shard_map/ppermute | solution.py:12
  67.1 3.1 %collective-permute-start.1 = (f32[3,1,128,128]{3,2,1,0:T(8,128)S(1)}, f32[3,1,128,128]{3,2,1,0:T(8,128)S(1)}, u32[]{:S(2)}, u32[]{:S(2)}) collective-permute-start(f32[3,1,128,128]{3,2,1,0:T(8,128)S(1)} %pad_maximum_fusion.1), channel_id=1, source_target_pairs={{0,64},{32,96},{64,0},{96,32},{128,192},{160,224},{192,128},{224,1... | collective-permute-start | bytes 589832 | tf_op jit(solution)/shard_map/ppermute | solution.py:12
  70.2 8.6 %collective-permute-done.1 = f32[3,1,128,128]{3,2,1,0:T(8,128)S(1)} collective-permute-done((f32[3,1,128,128]{3,2,1,0:T(8,128)S(1)}, f32[3,1,128,128]{3,2,1,0:T(8,128)S(1)}, u32[]{:S(2)}, u32[]{:S(2)}) %collective-permute-start.1) | collective-permute-done | bytes 196640 | tf_op jit(solution)/shard_map/ppermute | solution.py:12
  78.8 6.5 %collective-permute-start.2 = (f32[2,1,128,128]{3,2,1,0:T(8,128)S(1)}, f32[2,1,128,128]{3,2,1,0:T(8,128)S(1)}, u32[]{:S(2)}, u32[]{:S(2)}) collective-permute-start(f32[2,1,128,128]{3,2,1,0:T(8,128)S(1)} %pad_maximum_fusion.2), channel_id=1, source_target_pairs={{0,128},{32,160},{64,192},{96,224},{128,0},{160,32},{192,64},{224,... | collective-permute-start | bytes 393224 | tf_op jit(solution)/shard_map/ppermute | solution.py:12
  85.3 2.9 %collective-permute-done.2 = f32[2,1,128,128]{3,2,1,0:T(8,128)S(1)} collective-permute-done((f32[2,1,128,128]{3,2,1,0:T(8,128)S(1)}, f32[2,1,128,128]{3,2,1,0:T(8,128)S(1)}, u32[]{:S(2)}, u32[]{:S(2)}) %collective-permute-start.2) | collective-permute-done | bytes 131104 | tf_op jit(solution)/shard_map/ppermute | solution.py:12
  89.6 0.7 reshape.490
  90.3 7.9 %all-to-all-start.6 = ((bf16[32,2,1024]{2,1,0:T(2,128)(2,1)}), bf16[32,2,1024]{2,1,0:T(2,128)(2,1)S(1)}, u32[]{:S(2)}, u32[]{:S(2)}) async-start(bf16[32,2,1024]{2,1,0:T(2,128)(2,1)} %reshape.490), calls=%async_computation.6 | async-start | bytes 262144 | tf_op jit(solution)/shard_map/all_to_all | solution.py:156
  99.1 0.7 reshape.488
  101.3 0.7 reshape.486
  102.0 4.0 %all-to-all-done.6 = bf16[32,2,1024]{2,1,0:T(2,128)(2,1)S(1)} async-done(((bf16[32,2,1024]{2,1,0:T(2,128)(2,1)}), bf16[32,2,1024]{2,1,0:T(2,128)(2,1)S(1)}, u32[]{:S(2)}, u32[]{:S(2)}) %all-to-all-start.6) | async-done | bytes 131104 | tf_op jit(solution)/shard_map/all_to_all | solution.py:156
  105.9 3.9 %all-to-all-start.5 = ((bf16[32,2,1024]{2,1,0:T(2,128)(2,1)}), bf16[32,2,1024]{2,1,0:T(2,128)(2,1)S(1)}, u32[]{:S(2)}, u32[]{:S(2)}) async-start(bf16[32,2,1024]{2,1,0:T(2,128)(2,1)} %reshape.488), calls=%async_computation.5 | async-start | bytes 262144 | tf_op jit(solution)/shard_map/all_to_all | solution.py:153
  110.6 7.0 %all-to-all-done.5 = bf16[32,2,1024]{2,1,0:T(2,128)(2,1)S(1)} async-done(((bf16[32,2,1024]{2,1,0:T(2,128)(2,1)}), bf16[32,2,1024]{2,1,0:T(2,128)(2,1)S(1)}, u32[]{:S(2)}, u32[]{:S(2)}) %all-to-all-start.5) | async-done | bytes 131104 | tf_op jit(solution)/shard_map/all_to_all | solution.py:153
  117.6 3.9 %all-to-all-start.4 = ((bf16[32,2,1024]{2,1,0:T(2,128)(2,1)}), bf16[32,2,1024]{2,1,0:T(2,128)(2,1)S(1)}, u32[]{:S(2)}, u32[]{:S(2)}) async-start(bf16[32,2,1024]{2,1,0:T(2,128)(2,1)} %reshape.486), calls=%async_computation.4 | async-start | bytes 262144 | tf_op jit(solution)/shard_map/all_to_all | solution.py:150
  122.4 0.7 copy.73
  123.9 5.3 %all-to-all-done.4 = bf16[32,2,1024]{2,1,0:T(2,128)(2,1)S(1)} async-done(((bf16[32,2,1024]{2,1,0:T(2,128)(2,1)}), bf16[32,2,1024]{2,1,0:T(2,128)(2,1)S(1)}, u32[]{:S(2)}, u32[]{:S(2)}) %all-to-all-start.4) | async-done | bytes 131104 | tf_op jit(solution)/shard_map/all_to_all | solution.py:150
  (62 shorter events, 8.7 us)
Async XLA Ops:
  2.2 8.7 %copy-start = (bf16[16,32,128]{2,1,0:T(8,128)(2,1)S(1)}, bf16[16,32,128]{2,1,0:T(8,128)(2,1)}, u32[]{:S(2)}) copy-start(bf16[16,32,128]{2,1,0:T(8,128)(2,1)} %param.8) | copy-start | bytes 393220
  2.2 16.3 %all-to-all-start = ((bf16[16,32,128]{2,0,1:T(8,128)(2,1)}), bf16[16,32,128]{2,0,1:T(8,128)(2,1)S(1)}, u32[]{:S(2)}, u32[]{:S(2)}) async-start(bf16[16,32,128]{2,0,1:T(8,128)(2,1)} %copy.54), calls=%async_computation | async-start | bytes 262144 | tf_op jit(solution)/shard_map/all_to_all | solution.py:114
  11.7 10.8 %copy-start.1 = (bf16[16,32,128]{2,1,0:T(8,128)(2,1)S(1)}, bf16[16,32,128]{2,1,0:T(8,128)(2,1)}, u32[]{:S(2)}) copy-start(bf16[16,32,128]{2,1,0:T(8,128)(2,1)} %param.7) | copy-start | bytes 393220
  18.6 11.6 %all-to-all-start.1 = ((bf16[16,32,128]{2,0,1:T(8,128)(2,1)}), bf16[16,32,128]{2,0,1:T(8,128)(2,1)S(1)}, u32[]{:S(2)}, u32[]{:S(2)}) async-start(bf16[16,32,128]{2,0,1:T(8,128)(2,1)} %copy.55), calls=%async_computation.1 | async-start | bytes 262144 | tf_op jit(solution)/shard_map/all_to_all | solution.py:113
  23.2 10.9 %copy-start.3 = (f32[1,13,512]{2,0,1:T(1,128)S(1)}, f32[1,13,512]{2,0,1:T(1,128)}, u32[]{:S(2)}) copy-start(f32[1,13,512]{2,0,1:T(1,128)} %param.10) | copy-start | bytes 79876
  30.2 11.6 %all-to-all-start.2 = ((bf16[16,32,128]{2,0,1:T(8,128)(2,1)}), bf16[16,32,128]{2,0,1:T(8,128)(2,1)S(1)}, u32[]{:S(2)}, u32[]{:S(2)}) async-start(bf16[16,32,128]{2,0,1:T(8,128)(2,1)} %copy.58), calls=%async_computation.2 | async-start | bytes 262144 | tf_op jit(solution)/shard_map/all_to_all | solution.py:112
  34.1 0.9 copy-start.2
  41.8 11.6 %all-to-all-start.3 = ((bf16[16,32,128]{2,0,1:T(8,128)(2,1)}), bf16[16,32,128]{2,0,1:T(8,128)(2,1)S(1)}, u32[]{:S(2)}, u32[]{:S(2)}) async-start(bf16[16,32,128]{2,0,1:T(8,128)(2,1)} %copy.62), calls=%async_computation.3 | async-start | bytes 262144 | tf_op jit(solution)/shard_map/all_to_all | solution.py:111
  58.5 2.3 %copy-start.5 = (f32[512,512]{0,1:T(8,128)S(1)}, f32[512,512]{0,1:T(8,128)}, u32[]{:S(2)}) copy-start(f32[512,512]{0,1:T(8,128)} %get-tuple-element.48) | copy-start | bytes 3145732
  59.1 7.9 %collective-permute-start = (f32[4,1,128,128]{3,2,1,0:T(8,128)S(1)}, f32[4,1,128,128]{3,2,1,0:T(8,128)S(1)}, u32[]{:S(2)}, u32[]{:S(2)}) collective-permute-start(f32[4,1,128,128]{3,2,1,0:T(8,128)S(1)} %pad_maximum_fusion), channel_id=1, source_target_pairs={{0,32},{32,0},{64,96},{96,64},{128,160},{160,128},{192,224},{224,1... | collective-permute-start | bytes 786440 | tf_op jit(solution)/shard_map/ppermute | solution.py:12
  67.1 11.7 %collective-permute-start.1 = (f32[3,1,128,128]{3,2,1,0:T(8,128)S(1)}, f32[3,1,128,128]{3,2,1,0:T(8,128)S(1)}, u32[]{:S(2)}, u32[]{:S(2)}) collective-permute-start(f32[3,1,128,128]{3,2,1,0:T(8,128)S(1)} %pad_maximum_fusion.1), channel_id=1, source_target_pairs={{0,64},{32,96},{64,0},{96,32},{128,192},{160,224},{192,128},{224,1... | collective-permute-start | bytes 589832 | tf_op jit(solution)/shard_map/ppermute | solution.py:12
  78.8 9.5 %collective-permute-start.2 = (f32[2,1,128,128]{3,2,1,0:T(8,128)S(1)}, f32[2,1,128,128]{3,2,1,0:T(8,128)S(1)}, u32[]{:S(2)}, u32[]{:S(2)}) collective-permute-start(f32[2,1,128,128]{3,2,1,0:T(8,128)S(1)} %pad_maximum_fusion.2), channel_id=1, source_target_pairs={{0,128},{32,160},{64,192},{96,224},{128,0},{160,32},{192,64},{224,... | collective-permute-start | bytes 393224 | tf_op jit(solution)/shard_map/ppermute | solution.py:12
  90.3 15.6 %all-to-all-start.6 = ((bf16[32,2,1024]{2,1,0:T(2,128)(2,1)}), bf16[32,2,1024]{2,1,0:T(2,128)(2,1)S(1)}, u32[]{:S(2)}, u32[]{:S(2)}) async-start(bf16[32,2,1024]{2,1,0:T(2,128)(2,1)} %reshape.490), calls=%async_computation.6 | async-start | bytes 262144 | tf_op jit(solution)/shard_map/all_to_all | solution.py:156
  105.9 11.6 %all-to-all-start.5 = ((bf16[32,2,1024]{2,1,0:T(2,128)(2,1)}), bf16[32,2,1024]{2,1,0:T(2,128)(2,1)S(1)}, u32[]{:S(2)}, u32[]{:S(2)}) async-start(bf16[32,2,1024]{2,1,0:T(2,128)(2,1)} %reshape.488), calls=%async_computation.5 | async-start | bytes 262144 | tf_op jit(solution)/shard_map/all_to_all | solution.py:153
  109.9 0.7 copy-start.4
  117.6 11.6 %all-to-all-start.4 = ((bf16[32,2,1024]{2,1,0:T(2,128)(2,1)}), bf16[32,2,1024]{2,1,0:T(2,128)(2,1)S(1)}, u32[]{:S(2)}, u32[]{:S(2)}) async-start(bf16[32,2,1024]{2,1,0:T(2,128)(2,1)} %reshape.486), calls=%async_computation.4 | async-start | bytes 262144 | tf_op jit(solution)/shard_map/all_to_all | solution.py:150
where the time goes:
time: 131 us; the launch traced here: 130 us
  waiting for transfers between devices  59.8 us (46%)
  starting transfers between devices  47.6 us (36%)
  local copies, waits for them, and re-layouts  11.5 us (9%)
  other arithmetic  5.47 us (4%)
  matrix products  4.65 us (4%)
    ppermute x3, waiting for transfers between devices, partner(): return lax.ppermute(value, axis, pairs)  16.3 us
    ppermute x3, starting transfers between devices, partner(): return lax.ppermute(value, axis, pairs)  11.4 us
    unnamed x29, local copies, waits for them, and re-layouts  10.4 us
    all_to_all x1, starting transfers between devices, on_device(): lax.all_to_all(out_grad, 'head', split_axis=1, concat_axis=0, tiled=True)  8.71 us
    all_to_all x1, starting transfers between devices, on_device(): lax.all_to_all(value_total.astype(jnp.bfloat16), 'head', split_axis=0, co...  7.89 us
    all_to_all x1, waiting for transfers between devices, on_device(): lax.all_to_all(queries, 'head', split_axis=1, concat_axis=0, tiled=True)  7.31 us
    all_to_all x1, waiting for transfers between devices, on_device(): lax.all_to_all(values, 'head', split_axis=1, concat_axis=0, tiled=True)  6.99 us
    all_to_all x1, waiting for transfers between devices, on_device(): lax.all_to_all(key_total.astype(jnp.bfloat16), 'head', split_axis=0, conc...  6.98 us
  transfers between devices with their start and end apart: 10, of which 10 were waited for; matrix products, arithmetic and copies ran while one was open for 8% of the time, Pallas kernels for 0%

commit v1 on v0

v1 whole, which is shorter than its diff:
```python
import math

import jax
import jax.numpy as jnp
from jax import lax
from jax.experimental import pallas as pl
from jax.experimental.pallas import tpu as pltpu
from jax.sharding import PartitionSpec as P

HEAD_AXIS = "head"
SEQ_AXIS = "seq"
LANES = 128
F32 = jnp.float32
BF16 = jnp.bfloat16


def level_factor(degree, head_width):
    base_scale = 1.0 / math.sqrt(head_width)
    if degree == 0:
        return base_scale
    return base_scale * 2.0 ** (-(degree - 1) / 2.0)


def dot_nn(left, right):
    return lax.dot_general(left, right, (((1,), (0,)), ((), ())), preferred_element_type=F32)


def dot_nt(left, right):
    return lax.dot_general(left, right, (((1,), (1,)), ((), ())), preferred_element_type=F32)


def transposed(rows):
    return jnp.transpose(rows.astype(F32))


def seq_bit(degree):
    return (lax.axis_index(SEQ_AXIS) >> degree) & 1 == 1


def call(body, out_shape, operands, scratch=(), flops=0, moved=0):
    return pl.pallas_call(
        body,
        out_shape=out_shape,
        scratch_shapes=list(scratch),
        cost_estimate=pl.CostEstimate(flops=flops, bytes_accessed=moved, transcendentals=0),
    )(*operands)


def pack(members):
    rows, heads, width = members[0].shape
    count = len(members)

    def body(*refs):
        ins, out, wide = refs[:count], refs[count], refs[count + 1]
        for index in range(count):
            wide[index] = ins[index][...].astype(F32).reshape(rows * heads, width)
        for index in range(count):
            for head in range(heads):
                piece = wide[index, pl.ds(head, rows, stride=heads), :]
                out[head, index * rows : (index + 1) * rows, :] = piece.astype(BF16)

    size = count * rows * heads * width
    return call(
        body,
        jax.ShapeDtypeStruct((heads, count * rows, width), BF16),
        members,
        [pltpu.VMEM((count, rows * heads, width), F32)],
        moved=4 * size,
    )


def unpack(joined, count):
    heads, total, width = joined.shape
    rows = total // count

    def body(joined_ref, *refs):
        outs, wide = refs[:count], refs[count]
        for index in range(count):
            for head in range(heads):
                piece = joined_ref[head, index * rows : (index + 1) * rows, :]
                wide[index, pl.ds(head, rows, stride=heads), :] = piece.astype(F32)
        for index in range(count):
            outs[index][...] = wide[index].reshape(rows, heads, width).astype(BF16)

    size = count * rows * heads * width
    return call(
        body,
        tuple(jax.ShapeDtypeStruct((rows, heads, width), BF16) for _ in range(count)),
        (joined,),
        [pltpu.VMEM((count, rows * heads, width), F32)],
        moved=4 * size,
    )


def part(ref, index, chunk):
    sources, _, width = ref.shape
    return ref[:, index * chunk : (index + 1) * chunk, :].reshape(sources * chunk, width)


def block_states(rows_in, weights, chunk, first_far, far_count):
    width = rows_in.shape[2]

    def body(rows_ref, weight_ref, near_ref, wide_ref):
        query, key, value, grad = (part(rows_ref, index, chunk) for index in range(4))
        query_t = transposed(query)
        pair = dot_nn(transposed(key).astype(BF16), value)
        messages = []
        for degree in range(far_count):
            level = first_far + degree
            scale = level_factor(level, width) * weight_ref[level]
            state = dot_nn((scale * query_t).astype(BF16), grad)
            messages.append(jnp.where(seq_bit(degree), state, pair).astype(BF16))
        near_ref[0] = messages[0]
        near_ref[1] = messages[2]
        wide_ref[0] = messages[1]
        wide_ref[1] = messages[2]

    shape = jax.ShapeDtypeStruct((2, width, width), BF16)
    return call(body, (shape, shape), (rows_in, weights), flops=10**8, moved=10**6)


def near_terms(rows_in, weights, chunk, near_count):
    sources, _, width = rows_in.shape
    tokens = sources * chunk
    pieces = tokens // LANES
    inner = LANES.bit_length()

    def body(rows_ref, weight_ref, query_ref, key_ref, value_ref, grad_weight_ref):
        query, key, value, grad = (part(rows_ref, index, chunk) for index in range(4))
        scale = [level_factor(level, width) * weight_ref[level] for level in range(near_count)]
        source = lax.broadcasted_iota(jnp.int32, (LANES, LANES), 0)
        target = lax.broadcasted_iota(jnp.int32, (LANES, LANES), 1)
        crossed = source ^ target
        level_of = jnp.where(source <= target, 0, 64)
        for level in range(1, inner):
            level_of = level_of + (crossed >= 2 ** (level - 1)).astype(jnp.int32)
        masks = [level_of == level for level in range(inner)]
        sums = [[None] * pieces for _ in range(near_count)]
        key_t = transposed(key).astype(BF16)
        for low in range(pieces):
            begin = low * LANES
            span = tokens - begin
            scores = dot_nt(key[begin : begin + LANES], query[begin:])
            pulls = dot_nt(value[begin : begin + LANES], grad[begin:])
            product = scores * pulls
            inside = jnp.zeros((LANES, LANES), F32)
            corner = product[:, :LANES]
            for level in range(inner):
                row = scale[level][:, begin : begin + LANES]
                inside = jnp.where(masks[level], row, inside)
                sums[level][low] = jnp.sum(
                    jnp.where(masks[level], corner, 0.0), axis=0, keepdims=True
                )
            columns = [inside]
            for high in range(low + 1, pieces):
                level = (low ^ high).bit_length() + inner - 1
                left = (high - low) * LANES
                row = scale[level][:, high * LANES : (high + 1) * LANES]
                columns.append(jnp.broadcast_to(row, (LANES, LANES)))
                added = jnp.sum(product[:, left : left + LANES], axis=0, keepdims=True)
                held = sums[level][high]
                sums[level][high] = added if held is None else held + added
            weight = jnp.concatenate(columns, axis=1)
            scaled = (weight * scores).astype(BF16)
            pulled = (weight * pulls).astype(BF16)
            value_ref[begin : begin + LANES, :] = dot_nn(scaled, grad[begin:])
            key_ref[begin : begin + LANES, :] = dot_nn(pulled, query[begin:])
            partial = dot_nn(key_t[:, begin : begin + LANES], pulled)
            if low == 0:
                query_ref[...] = partial
            else:
                query_ref[:, begin:] = query_ref[:, begin:] + partial
        zero = jnp.zeros((1, LANES), F32)
        for level in range(near_count):
            row = jnp.concatenate([zero if item is None else item for item in sums[level]], axis=1)
            grad_weight_ref[level] = level_factor(level, width) * row

    return call(
        body,
        (
            jax.ShapeDtypeStruct((width, tokens), F32),
            jax.ShapeDtypeStruct((tokens, width), F32),
            jax.ShapeDtypeStruct((tokens, width), F32),
            jax.ShapeDtypeStruct((near_count, 1, tokens), F32),
        ),
        (rows_in, weights),
        flops=4 * 10**8,
        moved=3 * 10**6,
    )


def join_far(rows_in, weights, near, received, chunk, first_far, far_count):
    sources, _, width = rows_in.shape
    tokens = sources * chunk
    levels = weights.shape[0]
    query_near, key_near, value_near, weight_near = near

    def body(
        rows_ref,
        weight_ref,
        query_ref,
        key_ref,
        value_ref,
        near_weight_ref,
        first_ref,
        second_ref,
        third_ref,
        fourth_ref,
        out_ref,
        grad_weight_ref,
    ):
        query, key, value, grad = (part(rows_ref, index, chunk) for index in range(4))
        sums = [
            first_ref[0].astype(F32),
            second_ref[0].astype(F32) + third_ref[0].astype(F32),
            fourth_ref[0].astype(F32),
        ]
        query_t = transposed(query)
        total = query_ref[...]
        upper = jnp.zeros((width, width), F32)
        for degree in range(far_count):
            level = first_far + degree
            bit = seq_bit(degree)
            lower = jnp.where(bit, sums[degree], 0.0).astype(BF16)
            upper = upper + jnp.where(bit, 0.0, sums[degree])
            update = dot_nt(lower, grad)
            factor = level_factor(level, width)
            total = total + (factor * weight_ref[level]) * update
            grad_weight_ref[level] = factor * jnp.sum(query_t * update, axis=0, keepdims=True)
        for level in range(first_far):
            grad_weight_ref[level] = near_weight_ref[level]
        upper = upper.astype(BF16)
        results = (
            jnp.transpose(total),
            key_ref[...] + dot_nt(value, upper),
            value_ref[...] + dot_nn(key, upper),
        )
        for index, result in enumerate(results):
            out_ref[:, index * chunk : (index + 1) * chunk, :] = result.astype(BF16).reshape(
                sources, chunk, width
            )

    return call(
        body,
        (
            jax.ShapeDtypeStruct((sources, 3 * chunk, width), BF16),
            jax.ShapeDtypeStruct((levels, 1, tokens), F32),
        ),
        (rows_in, weights, query_near, key_near, value_near, weight_near, *received),
        flops=2 * 10**8,
        moved=3 * 10**6,
    )


def partner(value, mask):
    size = lax.axis_size(SEQ_AXIS)
    return lax.ppermute(value, SEQ_AXIS, [(place, place ^ mask) for place in range(size)])


def on_device(queries, keys, values, out_grad, level_weights):
    chunk = queries.shape[0]
    weights = jnp.transpose(level_weights, (1, 0, 2))
    sent = pack((queries, keys, values, out_grad))
    rows = lax.all_to_all(sent, HEAD_AXIS, 0, 0, tiled=True)
    first_far = weights.shape[2].bit_length()
    far_count = weights.shape[0] - first_far
    near_pair, wide_pair = block_states(rows, weights, chunk, first_far, far_count)
    near = near_terms(rows, weights, chunk, first_far)
    first = partner(near_pair, 1)
    second = partner(wide_pair, 2)
    third = partner(wide_pair, 3)
    quad = near_pair[1:] + first[1:] + second[1:] + third[1:]
    fourth = partner(quad, 7)
    joined, grad_weights = join_far(
        rows, weights, near, (first, second, third, fourth), chunk, first_far, far_count
    )
    back = lax.all_to_all(joined, HEAD_AXIS, 0, 0, tiled=True)
    query_out, key_out, value_out = unpack(back, 3)
    return (query_out, key_out, value_out, jnp.transpose(grad_weights, (1, 0, 2)))


def solution(mesh):
    rows = P((SEQ_AXIS, HEAD_AXIS), None, None)
    levels = P(HEAD_AXIS, None, SEQ_AXIS)
    return jax.shard_map(
        on_device,
        mesh=mesh,
        in_specs=(rows, rows, rows, rows, levels),
        out_specs=(rows, rows, rows, levels),
        check_vma=False,
    )
```

time: 131 us -> 66.1 us (0.50)
  waiting for transfers between devices: 59.8 us -> 6.88 us
  starting transfers between devices: 47.6 us -> 8.53 us
  blocking collectives: 0 us -> 35.7 us
  Pallas kernels: 0 us -> 12.5 us
  local copies, waits for them, and re-layouts: 11.5 us -> 0.62 us
  other arithmetic: 5.47 us -> 0.77 us
  matrix products: 4.65 us -> 0 us
    all_to_all x7 -> x0, waiting for transfers between devices: 43.5 us -> none  [the longest x1 7.31 us: on_device(): lax.all_to_all(queries, 'head', split_axis=1, concat_axis=0, tiled=True)]
    all_to_all x7 -> x0, starting transfers between devices: 36.2 us -> none  [the longest x1 8.71 us: on_device(): lax.all_to_all(out_grad, 'head', split_axis=1, concat_axis=0, tiled=True)]
    all_to_all x0 -> x2, blocking collectives: none -> 35.7 us  [the longest x1 20.1 us: on_device(): rows = lax.all_to_all(sent, HEAD_AXIS, 0, 0, tiled=True)]
    pallas_call x0 -> x5, Pallas kernels: none -> 12.5 us  [call(): pl.pallas_call(body, out_shape=out_shape, scratch_shapes=list(scratch), c...]
    unnamed x29 -> x8, local copies, waits for them, and re-layouts: 10.4 us -> 0.62 us
    ppermute x3 -> x4, waiting for transfers between devices: 16.3 us -> 6.88 us  [partner(): lax.ppermute(value, SEQ_AXIS, [(place, place ^ mask) for place in range(s...]
    dot_general x10 -> x0, matrix products: 4.65 us -> none  [the longest x1 1.75 us: near_terms(): jnp.einsum('thd,shd->hts', query_rows, key_rows, preferred_element_type=j...]
    reduce_sum x1 -> x0, other arithmetic: 3.1 us -> none  [near_terms(): chosen = jnp.sum(jnp.where(matching, product, 0.0), axis=2)]
  transfers between devices with their start and end apart: 10 -> 4, of which waited for: 10 -> 2; matrix products, arithmetic and copies ran while one was open for 8% -> 0% of each run, Pallas kernels for 0% -> 5%
where the time goes in v1:
time: 66.1 us; the launch traced here: 65.6 us
  blocking collectives  35.7 us (54%)
  Pallas kernels  12.5 us (19%)
  starting transfers between devices  8.53 us (13%)
  waiting for transfers between devices  6.88 us (10%)
  other arithmetic  0.77 us (1%)
  between operations  0.67 us (1%)
    all_to_all x1, blocking collectives, on_device(): rows = lax.all_to_all(sent, HEAD_AXIS, 0, 0, tiled=True)  20.1 us
    all_to_all x1, blocking collectives, on_device(): back = lax.all_to_all(joined, HEAD_AXIS, 0, 0, tiled=True)  15.6 us
    pallas_call x5, Pallas kernels, call(): pl.pallas_call(body, out_shape=out_shape, scratch_shapes=list(scratch), c...  12.5 us
    ppermute x4, starting transfers between devices, partner(): lax.ppermute(value, SEQ_AXIS, [(place, place ^ mask) for place in range(s...  8.53 us
    ppermute x4, waiting for transfers between devices, partner(): lax.ppermute(value, SEQ_AXIS, [(place, place ^ mask) for place in range(s...  6.88 us
  transfers between devices with their start and end apart: 4, of which 2 were waited for; matrix products, arithmetic and copies ran while one was open for 0% of the time, Pallas kernels for 5%

profile of v1, /device:TPU:1, one launch (start us, length us, event | category | flops | bytes accessed | tf_op | source)
XLA Modules:
  0.0 65.6 jit_solution(14876164773333513708)
XLA Ops:
  0.6 2.5 %shard_map.84 = bf16[32,64,128]{2,1,0:T(8,128)(2,1)} custom-call(bf16[16,32,128]{2,1,0:T(8,128)(2,1)} %refs_0_.1, bf16[16,32,128]{2,1,0:T(8,128)(2,1)} %refs_1_.1, bf16[16,32,128]{2,1,0:T(8,128)(2,1)} %refs_2_.1, bf16[16,32,128]{2,1,0:T(8,128)(2,1)} %refs_3_.1), custom_call_target="tpu_custom_call" | custom-call | bytes 1048576 | tf_op jit(solution)/shard_map/pallas_call | solution.py:41
  3.1 20.1 %all_to_all.10.rows_ref = bf16[32,64,128]{2,1,0:T(8,128)(2,1)} all-to-all(bf16[32,64,128]{2,1,0:T(8,128)(2,1)} %shard_map.84), channel_id=1, replica_groups=mesh['seq'=8,'head'=32] {'head'}, dimensions={0} | all-to-all | bytes 1048576 | tf_op jit(solution)/shard_map/all_to_all | solution.py:264
  23.3 2.1 %shard_map.86 = (bf16[2,128,128]{2,1,0:T(8,128)(2,1)}, bf16[2,128,128]{2,1,0:T(8,128)(2,1)}) custom-call(bf16[32,64,128]{2,1,0:T(8,128)(2,1)} %all_to_all.10.rows_ref, f32[13,1,512]{2,1,0:T(1,128)} %bitcast.2), custom_call_target="tpu_custom_call" | custom-call | flops 100000000 | bytes 1000000 | tf_op jit(solution)/shard_map/pallas_call | solution.py:41
  25.3 1.6 %collective-permute-start = (bf16[2,128,128]{2,1,0:T(8,128)(2,1)}, bf16[2,128,128]{2,1,0:T(8,128)(2,1)S(1)}, u32[]{:S(2)}, u32[]{:S(2)}) collective-permute-start(bf16[2,128,128]{2,1,0:T(8,128)(2,1)} %get-tuple-element.19), channel_id=1, source_target_pairs={{0,32},{32,0},{64,96},{96,64},{128,160},{160,128},{192,224},{224,1... | collective-permute-start | bytes 196616 | tf_op jit(solution)/shard_map/ppermute | solution.py:257
  26.9 2.7 %collective-permute-start.2 = (bf16[2,128,128]{2,1,0:T(8,128)(2,1)}, bf16[2,128,128]{2,1,0:T(8,128)(2,1)S(1)}, u32[]{:S(2)}, u32[]{:S(2)}) collective-permute-start(bf16[2,128,128]{2,1,0:T(8,128)(2,1)} %get-tuple-element.20), channel_id=1, source_target_pairs={{0,96},{32,64},{64,32},{96,0},{128,224},{160,192},{192,160},{224,1... | collective-permute-start | bytes 196616 | tf_op jit(solution)/shard_map/ppermute | solution.py:257
  29.7 0.3 collective-permute-start.1
  29.9 0.0 collective-permute-done.first_ref
  29.9 0.0 copy-start
  29.9 3.3 %collective-permute-done.2.third_ref = bf16[2,128,128]{2,1,0:T(8,128)(2,1)S(1)} collective-permute-done((bf16[2,128,128]{2,1,0:T(8,128)(2,1)}, bf16[2,128,128]{2,1,0:T(8,128)(2,1)S(1)}, u32[]{:S(2)}, u32[]{:S(2)}) %collective-permute-start.2) | collective-permute-done | bytes 65568 | tf_op jit(solution)/shard_map/ppermute | solution.py:257
  33.2 0.0 copy-start.1
  33.2 3.6 %collective-permute-done.1.second_ref = bf16[2,128,128]{2,1,0:T(8,128)(2,1)S(1)} collective-permute-done((bf16[2,128,128]{2,1,0:T(8,128)(2,1)}, bf16[2,128,128]{2,1,0:T(8,128)(2,1)S(1)}, u32[]{:S(2)}, u32[]{:S(2)}) %collective-permute-start.1) | collective-permute-done | bytes 65568 | tf_op jit(solution)/shard_map/ppermute | solution.py:257
  36.8 0.0 copy-start.2
  36.8 0.8 %slice_add_fusion = bf16[1,128,128]{2,1,0:T(8,128)(2,1)S(1)} fusion(bf16[2,128,128]{2,1,0:T(8,128)(2,1)S(1)} %collective-permute-done.2.third_ref, bf16[2,128,128]{2,1,0:T(8,128)(2,1)S(1)} %collective-permute-done.1.second_ref, bf16[2,128,128]{2,1,0:T(8,128)(2,1)S(1)} %collective-permute-done.first_ref, bf16[2,128,128]{2,1,0:T(8,128)(2,1)} %get-tuple-element.19), kind=kLoop, calls=%fused_computation | loop fusion | flops 49152 | bytes 163840 | tf_op jit(solution)/shard_map/add | solution.py:272
  37.6 0.0 copy-done
  37.6 0.0 copy-done.1
  37.6 3.9 %collective-permute-start.3 = (bf16[1,128,128]{2,1,0:T(8,128)(2,1)S(1)}, bf16[1,128,128]{2,1,0:T(8,128)(2,1)S(1)}, u32[]{:S(2)}, u32[]{:S(2)}) collective-permute-start(bf16[1,128,128]{2,1,0:T(8,128)(2,1)S(1)} %slice_add_fusion), channel_id=1, source_target_pairs={{0,224},{32,192},{64,160},{96,128},{128,96},{160,64},{192,32},{224... | collective-permute-start | bytes 98312 | tf_op jit(solution)/shard_map/ppermute | solution.py:257
  41.5 3.1 %shard_map.85 = (f32[128,512]{1,0:T(8,128)}, f32[512,128]{1,0:T(8,128)}, f32[512,128]{1,0:T(8,128)}, f32[10,1,512]{2,1,0:T(1,128)}) custom-call(bf16[32,64,128]{2,1,0:T(8,128)(2,1)} %all_to_all.10.rows_ref, f32[13,1,512]{2,1,0:T(1,128)} %bitcast.3), custom_call_target="tpu_custom_call" | custom-call | flops 400000000 | bytes 3000000 | tf_op jit(solution)/shard_map/pallas_call | solution.py:41
  44.6 0.0 copy-done.2
  44.6 0.0 collective-permute-done.3.fourth_ref
  44.6 0.0 copy-start.3
  44.7 0.6 copy-done.3
  45.3 2.4 %shard_map.87 = (bf16[32,48,128]{2,1,0:T(8,128)(2,1)}, f32[13,1,512]{2,1,0:T(1,128)}) custom-call(bf16[32,64,128]{2,1,0:T(8,128)(2,1)} %all_to_all.10.rows_ref, f32[13,1,512]{2,1,0:T(1,128)} %bitcast.4, f32[128,512]{1,0:T(8,128)} %get-tuple-element.15.query_ref, f32[512,128]{1,0:T(8,128)} %get-tuple-element.16.key_ref, ...), custom_call_target="tpu_custom_call" | custom-call | flops 200000000 | bytes 3000000 | tf_op jit(solution)/shard_map/pallas_call | solution.py:41
  47.7 15.6 %all_to_all.11.joined_ref = bf16[32,48,128]{2,1,0:T(8,128)(2,1)} all-to-all(bf16[32,48,128]{2,1,0:T(8,128)(2,1)} %get-tuple-element.21), channel_id=1, replica_groups=mesh['seq'=8,'head'=32] {'head'}, dimensions={0} | all-to-all | bytes 786432 | tf_op jit(solution)/shard_map/all_to_all | solution.py:277
  63.3 2.4 %shard_map.88 = (bf16[16,32,128]{2,1,0:T(8,128)(2,1)}, bf16[16,32,128]{2,1,0:T(8,128)(2,1)}, bf16[16,32,128]{2,1,0:T(8,128)(2,1)}) custom-call(bf16[32,48,128]{2,1,0:T(8,128)(2,1)} %all_to_all.11.joined_ref), custom_call_target="tpu_custom_call" | custom-call | bytes 786432 | tf_op jit(solution)/shard_map/pallas_call | solution.py:41
Async XLA Ops:
  25.3 4.6 %collective-permute-start = (bf16[2,128,128]{2,1,0:T(8,128)(2,1)}, bf16[2,128,128]{2,1,0:T(8,128)(2,1)S(1)}, u32[]{:S(2)}, u32[]{:S(2)}) collective-permute-start(bf16[2,128,128]{2,1,0:T(8,128)(2,1)} %get-tuple-element.19), channel_id=1, source_target_pairs={{0,32},{32,0},{64,96},{96,64},{128,160},{160,128},{192,224},{224,1... | collective-permute-start | bytes 196616 | tf_op jit(solution)/shard_map/ppermute | solution.py:257
  26.9 6.3 %collective-permute-start.2 = (bf16[2,128,128]{2,1,0:T(8,128)(2,1)}, bf16[2,128,128]{2,1,0:T(8,128)(2,1)S(1)}, u32[]{:S(2)}, u32[]{:S(2)}) collective-permute-start(bf16[2,128,128]{2,1,0:T(8,128)(2,1)} %get-tuple-element.20), channel_id=1, source_target_pairs={{0,96},{32,64},{64,32},{96,0},{128,224},{160,192},{192,160},{224,1... | collective-permute-start | bytes 196616 | tf_op jit(solution)/shard_map/ppermute | solution.py:257
  29.7 7.2 %collective-permute-start.1 = (bf16[2,128,128]{2,1,0:T(8,128)(2,1)}, bf16[2,128,128]{2,1,0:T(8,128)(2,1)S(1)}, u32[]{:S(2)}, u32[]{:S(2)}) collective-permute-start(bf16[2,128,128]{2,1,0:T(8,128)(2,1)} %get-tuple-element.20), channel_id=1, source_target_pairs={{0,64},{32,96},{64,0},{96,32},{128,192},{160,224},{192,128},{224,1... | collective-permute-start | bytes 196616 | tf_op jit(solution)/shard_map/ppermute | solution.py:257
  29.9 7.7 %copy-start = (bf16[2,128,128]{2,1,0:T(8,128)(2,1)}, bf16[2,128,128]{2,1,0:T(8,128)(2,1)S(1)}, u32[]{:S(2)}) copy-start(bf16[2,128,128]{2,1,0:T(8,128)(2,1)S(1)} %collective-permute-done.first_ref) | copy-start | bytes 196612
  33.2 4.4 %copy-start.1 = (bf16[2,128,128]{2,1,0:T(8,128)(2,1)}, bf16[2,128,128]{2,1,0:T(8,128)(2,1)S(1)}, u32[]{:S(2)}) copy-start(bf16[2,128,128]{2,1,0:T(8,128)(2,1)S(1)} %collective-permute-done.2.third_ref) | copy-start | bytes 196612
  36.8 7.8 %copy-start.2 = (bf16[2,128,128]{2,1,0:T(8,128)(2,1)}, bf16[2,128,128]{2,1,0:T(8,128)(2,1)S(1)}, u32[]{:S(2)}) copy-start(bf16[2,128,128]{2,1,0:T(8,128)(2,1)S(1)} %collective-permute-done.1.second_ref) | copy-start | bytes 196612
  37.6 7.0 %collective-permute-start.3 = (bf16[1,128,128]{2,1,0:T(8,128)(2,1)S(1)}, bf16[1,128,128]{2,1,0:T(8,128)(2,1)S(1)}, u32[]{:S(2)}, u32[]{:S(2)}) collective-permute-start(bf16[1,128,128]{2,1,0:T(8,128)(2,1)S(1)} %slice_add_fusion), channel_id=1, source_target_pairs={{0,224},{32,192},{64,160},{96,128},{128,96},{160,64},{192,32},{224... | collective-permute-start | bytes 98312 | tf_op jit(solution)/shard_map/ppermute | solution.py:257
  44.6 0.6 copy-start.3

commit v2 on v1

--- a/solution.py
+++ b/solution.py
@@ -7,6 +7,7 @@
 from jax.experimental.pallas import tpu as pltpu
 from jax.sharding import PartitionSpec as P
 
+
 HEAD_AXIS = "head"
 SEQ_AXIS = "seq"
 LANES = 128
@@ -37,11 +38,24 @@
     return (lax.axis_index(SEQ_AXIS) >> degree) & 1 == 1
 
 
-def call(body, out_shape, operands, scratch=(), flops=0, moved=0):
+def call(
+    body,
+    out_shape,
+    operands,
+    scratch=(),
+    flops=0,
+    moved=0,
+    in_space=pltpu.VMEM,
+    out_space=pltpu.VMEM,
+    limit=16 * 2**20,
+):
     return pl.pallas_call(
         body,
         out_shape=out_shape,
+        in_specs=[pl.BlockSpec(memory_space=in_space)] * len(operands),
+        out_specs=jax.tree.map(lambda _: pl.BlockSpec(memory_space=out_space), out_shape),
         scratch_shapes=list(scratch),
+        compiler_params=pltpu.CompilerParams(vmem_limit_bytes=limit),
         cost_estimate=pl.CostEstimate(flops=flops, bytes_accessed=moved, transcendentals=0),
     )(*operands)
 
@@ -51,10 +65,17 @@
     count = len(members)
 
     def body(*refs):
-        ins, out, wide = refs[:count], refs[count], refs[count + 1]
+        ins, out = refs[:count], refs[count]
+        narrow, wide, sems = refs[count + 1 :]
+        copies = [
+            pltpu.make_async_copy(ins[index], narrow.at[index], sems.at[index])
+            for index in range(count)
+        ]
+        for copy in copies:
+            copy.start()
         for index in range(count):
-            wide[index] = ins[index][...].astype(F32).reshape(rows * heads, width)
-        for index in range(count):
+            copies[index].wait()
+            wide[index] = narrow[index].astype(F32).reshape(rows * heads, width)
             for head in range(heads):
                 piece = wide[index, pl.ds(head, rows, stride=heads), :]
                 out[head, index * rows : (index + 1) * rows, :] = piece.astype(BF16)
@@ -64,8 +85,14 @@
         body,
         jax.ShapeDtypeStruct((heads, count * rows, width), BF16),
         members,
-        [pltpu.VMEM((count, rows * heads, width), F32)],
+        [
+            pltpu.VMEM((count, rows, heads, width), BF16),
+            pltpu.VMEM((count, rows * heads, width), F32),
+            pltpu.SemaphoreType.DMA((count,)),
+        ],
         moved=4 * size,
+        in_space=pltpu.HBM,
+        limit=63 * 2**20,
     )
 
 
@@ -74,21 +101,32 @@
     rows = total // count
 
     def body(joined_ref, *refs):
-        outs, wide = refs[:count], refs[count]
+        outs = refs[:count]
+        narrow, wide, sems = refs[count:]
+        copies = []
         for index in range(count):
             for head in range(heads):
                 piece = joined_ref[head, index * rows : (index + 1) * rows, :]
                 wide[index, pl.ds(head, rows, stride=heads), :] = piece.astype(F32)
-        for index in range(count):
-            outs[index][...] = wide[index].reshape(rows, heads, width).astype(BF16)
+            narrow[index] = wide[index].reshape(rows, heads, width).astype(BF16)
+            copy = pltpu.make_async_copy(narrow.at[index], outs[index], sems.at[index])
+            copy.start()
+            copies.append(copy)
+        for copy in copies:
+            copy.wait()
 
     size = count * rows * heads * width
     return call(
         body,
         tuple(jax.ShapeDtypeStruct((rows, heads, width), BF16) for _ in range(count)),
         (joined,),
-        [pltpu.VMEM((count, rows * heads, width), F32)],
+        [
+            pltpu.VMEM((count, rows, heads, width), BF16),
+            pltpu.VMEM((count, rows * heads, width), F32),
+            pltpu.SemaphoreType.DMA((count,)),
+        ],
         moved=4 * size,
+        out_space=pltpu.HBM,
     )
 
 
@@ -100,7 +138,7 @@
 def block_states(rows_in, weights, chunk, first_far, far_count):
     width = rows_in.shape[2]
 
-    def body(rows_ref, weight_ref, near_ref, wide_ref):
+    def body(rows_ref, weight_ref, *message_refs):
         query, key, value, grad = (part(rows_ref, index, chunk) for index in range(4))
         query_t = transposed(query)
         pair = dot_nn(transposed(key).astype(BF16), value)
@@ -110,13 +148,12 @@
             scale = level_factor(level, width) * weight_ref[level]
             state = dot_nn((scale * query_t).astype(BF16), grad)
             messages.append(jnp.where(seq_bit(degree), state, pair).astype(BF16))
-        near_ref[0] = messages[0]
-        near_ref[1] = messages[2]
-        wide_ref[0] = messages[1]
-        wide_ref[1] = messages[2]
-
-    shape = jax.ShapeDtypeStruct((2, width, width), BF16)
-    return call(body, (shape, shape), (rows_in, weights), flops=10**8, moved=10**6)
+        for refs, groups in zip(message_refs, SENT):
+            for slot, degree in enumerate(groups):
+                refs[slot] = messages[degree]
+
+    shapes = tuple(jax.ShapeDtypeStruct((len(groups), width, width), BF16) for groups in SENT)
+    return call(body, shapes, (rows_in, weights), flops=10**8, moved=10**6)
 
 
 def near_terms(rows_in, weights, chunk, near_count):
@@ -139,7 +176,6 @@
         key_t = transposed(key).astype(BF16)
         for low in range(pieces):
             begin = low * LANES
-            span = tokens - begin
             scores = dot_nt(key[begin : begin + LANES], query[begin:])
             pulls = dot_nt(value[begin : begin + LANES], grad[begin:])
             product = scores * pulls
@@ -202,19 +238,17 @@
         key_ref,
         value_ref,
         near_weight_ref,
-        first_ref,
-        second_ref,
-        third_ref,
-        fourth_ref,
-        out_ref,
-        grad_weight_ref,
+        *refs,
     ):
+        message_refs, (out_ref, grad_weight_ref) = refs[:-2], refs[-2:]
         query, key, value, grad = (part(rows_ref, index, chunk) for index in range(4))
-        sums = [
-            first_ref[0].astype(F32),
-            second_ref[0].astype(F32) + third_ref[0].astype(F32),
-            fourth_ref[0].astype(F32),
-        ]
+        sums = []
+        for sources_of in TAKEN:
+            terms = [message_refs[place][slot].astype(F32) for place, slot in sources_of]
+            total = terms[0]
+            for term in terms[1:]:
+                total = total + term
+            sums.append(total)
         query_t = transposed(query)
         total = query_ref[...]
         upper = jnp.zeros((width, width), F32)
@@ -264,24 +298,33 @@
     rows = lax.all_to_all(sent, HEAD_AXIS, 0, 0, tiled=True)
     first_far = weights.shape[2].bit_length()
     far_count = weights.shape[0] - first_far
-    near_pair, wide_pair = block_states(rows, weights, chunk, first_far, far_count)
+    messages = block_states(rows, weights, chunk, first_far, far_count)
     near = near_terms(rows, weights, chunk, first_far)
-    first = partner(near_pair, 1)
-    second = partner(wide_pair, 2)
-    third = partner(wide_pair, 3)
-    quad = near_pair[1:] + first[1:] + second[1:] + third[1:]
-    fourth = partner(quad, 7)
+    received = exchange(messages)
     joined, grad_weights = join_far(
-        rows, weights, near, (first, second, third, fourth), chunk, first_far, far_count
+        rows, weights, near, received, chunk, first_far, far_count
     )
     back = lax.all_to_all(joined, HEAD_AXIS, 0, 0, tiled=True)
     query_out, key_out, value_out = unpack(back, 3)
     return (query_out, key_out, value_out, jnp.transpose(grad_weights, (1, 0, 2)))
 
 
+SENT = ((0, 2), (1,), (2,))
+TAKEN = (((0, 0),), ((1, 0), (2, 0)), ((3, 0),))
+
+
+def exchange(messages):
+    a, b, c = messages
+    near, mid, far = partner(a, 1), partner(c, 2), partner(c, 3)
+    second, third = partner(b, 2), partner(b, 3)
+    quad = c + near[1:] + mid + far
+    return (near, second, third, partner(quad, 7))
+
+
 def solution(mesh):
     rows = P((SEQ_AXIS, HEAD_AXIS), None, None)
     levels = P(HEAD_AXIS, None, SEQ_AXIS)
+
     return jax.shard_map(
         on_device,
         mesh=mesh,

time: 66.1 us -> 56.4 us (0.85)
  Pallas kernels: 12.5 us -> 6.21 us
  waiting for transfers between devices: 6.88 us -> 1.8 us
  starting transfers between devices: 8.53 us -> 11 us
  other arithmetic: 0.77 us -> 0.01 us
  blocking collectives: 35.7 us -> 36.4 us
    pallas_call x5, Pallas kernels: 12.5 us -> 6.21 us  [call(): pl.pallas_call(body, out_shape=out_shape, in_specs=[pl.BlockSpec(memory_s...]
    ppermute x4 -> x6, waiting for transfers between devices: 6.88 us -> 1.8 us  [partner(): lax.ppermute(value, SEQ_AXIS, [(place, place ^ mask) for place in range(s...]
    ppermute x4 -> x6, starting transfers between devices: 8.53 us -> 11 us  [partner(): lax.ppermute(value, SEQ_AXIS, [(place, place ^ mask) for place in range(s...]
    all_to_all x1, blocking collectives: 15.6 us -> 16.4 us  [on_device(): back = lax.all_to_all(joined, HEAD_AXIS, 0, 0, tiled=True)]
    add x1, other arithmetic: 0.77 us -> 0.01 us  [exchange(): quad = c + near[1:] + mid + far]
  transfers between devices with their start and end apart: 4 -> 6, of which waited for: 2 -> 2; matrix products, arithmetic and copies ran while one was open for 0% -> 0% of each run, Pallas kernels for 5% -> 2%
where the time goes in v2:
time: 56.4 us; the launch traced here: 56.1 us
  blocking collectives  36.4 us (65%)
  starting transfers between devices  11 us (20%)
  Pallas kernels  6.21 us (11%)
  waiting for transfers between devices  1.8 us (3%)
  between operations  0.69 us (1%)
    all_to_all x1, blocking collectives, on_device(): rows = lax.all_to_all(sent, HEAD_AXIS, 0, 0, tiled=True)  20 us
    all_to_all x1, blocking collectives, on_device(): back = lax.all_to_all(joined, HEAD_AXIS, 0, 0, tiled=True)  16.4 us
    ppermute x6, starting transfers between devices, partner(): lax.ppermute(value, SEQ_AXIS, [(place, place ^ mask) for place in range(s...  11 us
    pallas_call x5, Pallas kernels, call(): pl.pallas_call(body, out_shape=out_shape, in_specs=[pl.BlockSpec(memory_s...  6.21 us
    ppermute x6, waiting for transfers between devices, partner(): lax.ppermute(value, SEQ_AXIS, [(place, place ^ mask) for place in range(s...  1.8 us
  transfers between devices with their start and end apart: 6, of which 2 were waited for; matrix products, arithmetic and copies ran while one was open for 0% of the time, Pallas kernels for 2%

profile of v2, /device:TPU:1, one launch (start us, length us, event | category | flops | bytes accessed | tf_op | source)
XLA Modules:
  0.0 56.1 jit_solution(3831747901182702684)
XLA Ops:
  0.6 2.4 %shard_map.84 = bf16[32,64,128]{2,1,0:T(8,128)(2,1)} custom-call(bf16[16,32,128]{2,1,0:T(8,128)(2,1)} %refs_0_.1, bf16[16,32,128]{2,1,0:T(8,128)(2,1)} %refs_1_.1, bf16[16,32,128]{2,1,0:T(8,128)(2,1)} %refs_2_.1, bf16[16,32,128]{2,1,0:T(8,128)(2,1)} %refs_3_.1), custom_call_target="tpu_custom_call" | custom-call | bytes 1048576 | tf_op jit(solution)/shard_map/pallas_call | solution.py:52
  3.0 0.0 copy-start
  3.1 20.0 %all_to_all.10.rows_ref = bf16[32,64,128]{2,1,0:T(8,128)(2,1)S(1)} all-to-all(bf16[32,64,128]{2,1,0:T(8,128)(2,1)} %shard_map.84), channel_id=1, replica_groups=mesh['seq'=8,'head'=32] {'head'}, dimensions={0} | all-to-all | bytes 1048576 | tf_op jit(solution)/shard_map/all_to_all | solution.py:298
  23.1 0.0 copy-done
  23.1 0.4 shard_map.86
  23.4 1.7 %collective-permute-start = (bf16[2,128,128]{2,1,0:T(8,128)(2,1)S(1)}, bf16[2,128,128]{2,1,0:T(8,128)(2,1)S(1)}, u32[]{:S(2)}, u32[]{:S(2)}) collective-permute-start(bf16[2,128,128]{2,1,0:T(8,128)(2,1)S(1)} %get-tuple-element.20), channel_id=1, source_target_pairs={{0,32},{32,0},{64,96},{96,64},{128,160},{160,128},{192,224},{224,1... | collective-permute-start | bytes 196616 | tf_op jit(solution)/shard_map/ppermute | solution.py:291
  25.2 2.8 %collective-permute-start.4 = (bf16[1,128,128]{2,1,0:T(8,128)(2,1)S(1)}, bf16[1,128,128]{2,1,0:T(8,128)(2,1)S(1)}, u32[]{:S(2)}, u32[]{:S(2)}) collective-permute-start(bf16[1,128,128]{2,1,0:T(8,128)(2,1)S(1)} %get-tuple-element.22), channel_id=1, source_target_pairs={{0,96},{32,64},{64,32},{96,0},{128,224},{160,192},{192,160},{224,1... | collective-permute-start | bytes 98312 | tf_op jit(solution)/shard_map/ppermute | solution.py:291
  28.0 0.2 collective-permute-start.3
  28.1 2.4 %collective-permute-start.2 = (bf16[1,128,128]{2,1,0:T(8,128)(2,1)S(1)}, bf16[1,128,128]{2,1,0:T(8,128)(2,1)S(1)}, u32[]{:S(2)}, u32[]{:S(2)}) collective-permute-start(bf16[1,128,128]{2,1,0:T(8,128)(2,1)S(1)} %get-tuple-element.21), channel_id=1, source_target_pairs={{0,96},{32,64},{64,32},{96,0},{128,224},{160,192},{192,160},{224,1... | collective-permute-start | bytes 98312 | tf_op jit(solution)/shard_map/ppermute | solution.py:291
  30.5 0.0 collective-permute-start.1
  30.5 0.0 collective-permute-done.4
  30.5 1.5 %collective-permute-done.3 = bf16[1,128,128]{2,1,0:T(8,128)(2,1)S(1)} collective-permute-done((bf16[1,128,128]{2,1,0:T(8,128)(2,1)S(1)}, bf16[1,128,128]{2,1,0:T(8,128)(2,1)S(1)}, u32[]{:S(2)}, u32[]{:S(2)}) %collective-permute-start.3) | collective-permute-done | bytes 32800 | tf_op jit(solution)/shard_map/ppermute | solution.py:291
  32.0 0.0 collective-permute-done.refs_0_
  32.0 3.9 %collective-permute-start.5 = (bf16[1,128,128]{2,1,0:T(8,128)(2,1)S(1)}, bf16[1,128,128]{2,1,0:T(8,128)(2,1)S(1)}, u32[]{:S(2)}, u32[]{:S(2)}) collective-permute-start(bf16[1,128,128]{2,1,0:T(8,128)(2,1)S(1)} %fusion.1), channel_id=1, source_target_pairs={{0,224},{32,192},{64,160},{96,128},{128,96},{160,64},{192,32},{224... | collective-permute-start | bytes 98312 | tf_op jit(solution)/shard_map/ppermute | solution.py:291
  35.9 1.2 %shard_map.85 = (f32[128,512]{1,0:T(8,128)S(1)}, f32[512,128]{1,0:T(8,128)S(1)}, f32[512,128]{1,0:T(8,128)S(1)}, f32[10,1,512]{2,1,0:T(1,128)S(1)}) custom-call(bf16[32,64,128]{2,1,0:T(8,128)(2,1)S(1)} %all_to_all.10.rows_ref, f32[13,1,512]{2,1,0:T(1,128)S(1)} %bitcast.3), custom_call_target="tpu_custom_call" | custom-call | flops 400000000 | bytes 3000000 | tf_op jit(solution)/shard_map/pallas_call | solution.py:52
  37.1 0.0 collective-permute-done.2.refs_2_
  37.1 0.0 collective-permute-done.1.refs_1_
  37.1 0.3 collective-permute-done.5.refs_3_
  37.5 0.9 %shard_map.87 = (bf16[32,48,128]{2,1,0:T(8,128)(2,1)S(1)}, f32[13,1,512]{2,1,0:T(1,128)}) custom-call(bf16[32,64,128]{2,1,0:T(8,128)(2,1)S(1)} %all_to_all.10.rows_ref, f32[13,1,512]{2,1,0:T(1,128)S(1)} %bitcast.4, f32[128,512]{1,0:T(8,128)S(1)} %get-tuple-element.16.query_ref, f32[512,128]{1,0:T(8,128)S(1)} %get-tuple-element.17.key_ref, ...), custom_call_target="tpu_custom_call" | custom-call | flops 200000000 | bytes 3000000 | tf_op jit(solution)/shard_map/pallas_call | solution.py:52
  38.4 16.4 %all_to_all.11.joined_ref = bf16[32,48,128]{2,1,0:T(8,128)(2,1)S(1)} all-to-all(bf16[32,48,128]{2,1,0:T(8,128)(2,1)S(1)} %get-tuple-element.23), channel_id=1, replica_groups=mesh['seq'=8,'head'=32] {'head'}, dimensions={0} | all-to-all | bytes 786432 | tf_op jit(solution)/shard_map/all_to_all | solution.py:307
  54.7 1.4 %shard_map.88 = (bf16[16,32,128]{2,1,0:T(8,128)(2,1)}, bf16[16,32,128]{2,1,0:T(8,128)(2,1)}, bf16[16,32,128]{2,1,0:T(8,128)(2,1)}) custom-call(bf16[32,48,128]{2,1,0:T(8,128)(2,1)S(1)} %all_to_all.11.joined_ref), custom_call_target="tpu_custom_call" | custom-call | bytes 786432 | tf_op jit(solution)/shard_map/pallas_call | solution.py:52
  (1 shorter events, 0.0 us)
Async XLA Ops:
  3.0 20.0 %copy-start = (f32[1,13,512]{2,0,1:T(1,128)S(1)}, f32[1,13,512]{2,0,1:T(1,128)}, u32[]{:S(2)}) copy-start(f32[1,13,512]{2,0,1:T(1,128)} %param.9) | copy-start | bytes 79876
  23.4 8.6 %collective-permute-start = (bf16[2,128,128]{2,1,0:T(8,128)(2,1)S(1)}, bf16[2,128,128]{2,1,0:T(8,128)(2,1)S(1)}, u32[]{:S(2)}, u32[]{:S(2)}) collective-permute-start(bf16[2,128,128]{2,1,0:T(8,128)(2,1)S(1)} %get-tuple-element.20), channel_id=1, source_target_pairs={{0,32},{32,0},{64,96},{96,64},{128,160},{160,128},{192,224},{224,1... | collective-permute-start | bytes 196616 | tf_op jit(solution)/shard_map/ppermute | solution.py:291
  25.2 5.4 %collective-permute-start.4 = (bf16[1,128,128]{2,1,0:T(8,128)(2,1)S(1)}, bf16[1,128,128]{2,1,0:T(8,128)(2,1)S(1)}, u32[]{:S(2)}, u32[]{:S(2)}) collective-permute-start(bf16[1,128,128]{2,1,0:T(8,128)(2,1)S(1)} %get-tuple-element.22), channel_id=1, source_target_pairs={{0,96},{32,64},{64,32},{96,0},{128,224},{160,192},{192,160},{224,1... | collective-permute-start | bytes 98312 | tf_op jit(solution)/shard_map/ppermute | solution.py:291
  28.0 4.0 %collective-permute-start.3 = (bf16[1,128,128]{2,1,0:T(8,128)(2,1)S(1)}, bf16[1,128,128]{2,1,0:T(8,128)(2,1)S(1)}, u32[]{:S(2)}, u32[]{:S(2)}) collective-permute-start(bf16[1,128,128]{2,1,0:T(8,128)(2,1)S(1)} %get-tuple-element.22), channel_id=1, source_target_pairs={{0,64},{32,96},{64,0},{96,32},{128,192},{160,224},{192,128},{224,1... | collective-permute-start | bytes 98312 | tf_op jit(solution)/shard_map/ppermute | solution.py:291
  28.1 9.0 %collective-permute-start.2 = (bf16[1,128,128]{2,1,0:T(8,128)(2,1)S(1)}, bf16[1,128,128]{2,1,0:T(8,128)(2,1)S(1)}, u32[]{:S(2)}, u32[]{:S(2)}) collective-permute-start(bf16[1,128,128]{2,1,0:T(8,128)(2,1)S(1)} %get-tuple-element.21), channel_id=1, source_target_pairs={{0,96},{32,64},{64,32},{96,0},{128,224},{160,192},{192,160},{224,1... | collective-permute-start | bytes 98312 | tf_op jit(solution)/shard_map/ppermute | solution.py:291
  30.5 6.6 %collective-permute-start.1 = (bf16[1,128,128]{2,1,0:T(8,128)(2,1)S(1)}, bf16[1,128,128]{2,1,0:T(8,128)(2,1)S(1)}, u32[]{:S(2)}, u32[]{:S(2)}) collective-permute-start(bf16[1,128,128]{2,1,0:T(8,128)(2,1)S(1)} %get-tuple-element.21), channel_id=1, source_target_pairs={{0,64},{32,96},{64,0},{96,32},{128,192},{160,224},{192,128},{224,1... | collective-permute-start | bytes 98312 | tf_op jit(solution)/shard_map/ppermute | solution.py:291
  32.0 5.5 %collective-permute-start.5 = (bf16[1,128,128]{2,1,0:T(8,128)(2,1)S(1)}, bf16[1,128,128]{2,1,0:T(8,128)(2,1)S(1)}, u32[]{:S(2)}, u32[]{:S(2)}) collective-permute-start(bf16[1,128,128]{2,1,0:T(8,128)(2,1)S(1)} %fusion.1), channel_id=1, source_target_pairs={{0,224},{32,192},{64,160},{96,128},{128,96},{160,64},{192,32},{224... | collective-permute-start | bytes 98312 | tf_op jit(solution)/shard_map/ppermute | solution.py:291
